TPU v7x, 32 devices: a whole 2x2x4 slice. The times are simulated.
32 devices in a mesh: img: 8 (over y, x, core), seq: 4 (over z).
Axes of the slice: x: 2, y: 2, z: 4, core: 2. Of those that a mesh axis runs over, the one named last changes fastest.
Arguments:
- x_big: bfloat16 [128, 200, 768], P(('img', 'seq')), may hold values from -6 to 6
- x_small: bfloat16 [512, 40, 768], P(('img', 'seq')), may hold values from -6 to 6
- mask_big: int32 [128, 200], P('img'), may hold values from 0 to 1, as said below
- mask_small: int32 [512, 40], P('img'), may hold values from 0 to 1, as said below
- ln1_gain: float32 [768], P('seq'), may hold values from 0.5 to 1.5
- ln1_bias: float32 [768], P('seq'), may hold values from -1.75 to 1.75
- w_qkv: float32 [768, 2304], P('img', 'seq'), may hold values from -0.21875 to 0.21875
- b_qv: float32 [1536], P('seq'), may hold values from -3 to 3
- w_out: float32 [768, 768], P('img', 'seq'), may hold values from -0.625 to 0.625
- b_out: float32 [768], P('seq'), may hold values from -1.75 to 1.75
- ln2_gain: float32 [768], P('seq'), may hold values from 0.5 to 1.5
- ln2_bias: float32 [768], P('seq'), may hold values from -1.75 to 1.75
- w_up: float32 [768, 3072], P('img', 'seq'), may hold values from -0.21875 to 0.21875
- b_up: float32 [3072], P('seq'), may hold values from -3 to 3
- w_down: float32 [3072, 768], P('img', 'seq'), may hold values from -0.109375 to 0.109375
- b_down: float32 [768], P('seq'), may hold values from -1.75 to 1.75
- dy_big: bfloat16 [128, 200, 768], P(('img', 'seq')), may hold values from -6 to 6
- dy_small: bfloat16 [512, 40, 768], P(('img', 'seq')), may hold values from -6 to 6
Outputs:
- y_big: bfloat16 [128, 200, 768], P(('img', 'seq'))
- y_small: bfloat16 [512, 40, 768], P(('img', 'seq'))
- dx_big: bfloat16 [128, 200, 768], P(('img', 'seq'))
- dx_small: bfloat16 [512, 40, 768], P(('img', 'seq'))
- g_ln1_gain: float32 [768], P('seq')
- g_ln1_bias: float32 [768], P('seq')
- g_w_qkv: float32 [768, 2304], P('img', 'seq')
- g_b_qv: float32 [1536], P('seq')
- g_w_out: float32 [768, 768], P('img', 'seq')
- g_b_out: float32 [768], P('seq')
- g_ln2_gain: float32 [768], P('seq')
- g_ln2_bias: float32 [768], P('seq')
- g_w_up: float32 [768, 3072], P('img', 'seq')
- g_b_up: float32 [3072], P('seq')
- g_w_down: float32 [3072, 768], P('img', 'seq')
- g_b_down: float32 [768], P('seq')
Inputs may be any that keep to these rules, and one draw needn't show every extreme that they name: `mask_big`: each 224px crop's mask is 1 on its first 175 to 200 slots and 0 after; some crop has all slots valid and some the fewest. `mask_small`: each 96px crop's mask is 1 on its first 35 to 40 slots and 0 after; some crop has all slots valid and some the fewest.
All inputs are finite; a program needn't handle non-finite values.
Results may differ from a plain program's by a relative error of at most 0.014.
Values may be sent and summed in bfloat16 or wider, within the bound.
A program may use at most 192 MiB of HBM per device.

v0:
```python
import jax
import jax.numpy as jnp
from jax import lax
from jax.sharding import PartitionSpec as P

HEADS = 12
HEAD_DIM = 64
AXES = ("img", "seq")
EPSILON = 1e-06
NEGATIVE = -1e30


def layer_norm(values, gain_vec, shift_vec):
    row_mean = jnp.mean(values, axis=-1, keepdims=True)
    centred = values - row_mean
    variance = jnp.mean(centred * centred, axis=-1, keepdims=True)
    return centred * lax.rsqrt(variance + EPSILON) * gain_vec + shift_vec


def gelu_exact(values):
    return jax.nn.gelu(values, approximate=False)


def head_scores(heads_in, key_valid):
    crop_count, length = (heads_in.shape[0], heads_in.shape[1])
    pieces = heads_in.reshape(crop_count, length, 3, HEADS, HEAD_DIM)
    queries, key_rows, value_rows = (pieces[:, :, 0], pieces[:, :, 1], pieces[:, :, 2])
    raw_scores = jnp.einsum(
        "cqhd,ckhd->chqk", queries, key_rows, preferred_element_type=jnp.float32
    )
    scores = jnp.where(key_valid[:, None, None, :] > 0, raw_scores * HEAD_DIM ** (-0.5), NEGATIVE)
    return (queries, key_rows, value_rows, scores)


def attend(heads_in, key_valid):
    crop_count, length = (heads_in.shape[0], heads_in.shape[1])
    queries, key_rows, value_rows, scores = head_scores(heads_in, key_valid)
    row_max = jnp.max(scores, axis=-1, keepdims=True)
    exponent = jnp.exp(scores - row_max)
    row_total = jnp.sum(exponent, axis=-1, keepdims=True)
    softmax_w = (exponent / row_total).astype(jnp.bfloat16)
    mixed_out = jnp.einsum(
        "chqk,ckhd->cqhd", softmax_w, value_rows, preferred_element_type=jnp.float32
    )
    log_total = row_max + jnp.log(row_total)
    return (mixed_out.astype(jnp.bfloat16).reshape(crop_count * length, -1), log_total)


def attend_back(heads_in, key_valid, log_total, grad_heads):
    crop_count, length = (heads_in.shape[0], heads_in.shape[1])
    queries, key_rows, value_rows, scores = head_scores(heads_in, key_valid)
    softmax_f = jnp.exp(scores - log_total)
    grad_mixed = grad_heads.reshape(crop_count, length, HEADS, HEAD_DIM)
    grad_soft = jnp.einsum(
        "cqhd,ckhd->chqk", grad_mixed, value_rows, preferred_element_type=jnp.float32
    )
    inner_sum = jnp.sum(softmax_f * grad_soft, axis=-1, keepdims=True)
    grad_raw = (softmax_f * (grad_soft - inner_sum) * HEAD_DIM ** (-0.5)).astype(jnp.bfloat16)
    grad_query = jnp.einsum(
        "chqk,ckhd->cqhd", grad_raw, key_rows, preferred_element_type=jnp.float32
    )
    grad_key = jnp.einsum("chqk,cqhd->ckhd", grad_raw, queries, preferred_element_type=jnp.float32)
    grad_value = jnp.einsum(
        "chqk,cqhd->ckhd",
        softmax_f.astype(jnp.bfloat16),
        grad_mixed,
        preferred_element_type=jnp.float32,
    )
    stacked = jnp.stack([grad_query, grad_key, grad_value], axis=2).astype(jnp.bfloat16)
    return stacked.reshape(crop_count * length, -1)


def gather_mats(mats):
    n_img, n_seq = (lax.axis_size("img"), lax.axis_size("seq"))
    flat = jnp.concatenate([m.astype(jnp.bfloat16).reshape(-1, 64) for m in mats], axis=0)
    whole = lax.all_gather(flat, AXES, axis=0, tiled=False)
    outs, at = ([], 0)
    for m in mats:
        rows = m.size // 64
        piece = whole[:, at : at + rows].reshape((n_img, n_seq) + m.shape)
        at += rows
        if m.ndim == 2:
            piece = piece.transpose(0, 2, 1, 3).reshape(n_img * m.shape[0], n_seq * m.shape[1])
        else:
            piece = piece[0].reshape(-1)
        outs.append(piece)
    return outs


def scatter_mats(mats):
    n_img, n_seq = (lax.axis_size("img"), lax.axis_size("seq"))
    blocks = []
    for m in mats:
        rows, cols = (m.shape[0] // n_img, m.shape[1] // n_seq)
        b = m.astype(jnp.bfloat16).reshape(n_img, rows, n_seq, cols).transpose(0, 2, 1, 3)
        blocks.append(b.reshape(n_img * n_seq, -1, 128))
    flat = jnp.concatenate(blocks, axis=1)
    mine = lax.psum_scatter(flat, AXES, scatter_dimension=0, tiled=False)
    outs, at = ([], 0)
    for m, b in zip(mats, blocks):
        piece = mine[at : at + b.shape[1]]
        at += b.shape[1]
        outs.append(piece.reshape(m.shape[0] // n_img, m.shape[1] // n_seq).astype(jnp.float32))
    return outs


def body(
    x_big,
    x_small,
    mask_big,
    mask_small,
    ln1_gain,
    ln1_bias,
    w_qkv,
    b_qv,
    w_out,
    b_out,
    ln2_gain,
    ln2_bias,
    w_up,
    b_up,
    w_down,
    b_down,
    dy_big,
    dy_small,
):
    n_seq = lax.axis_size("seq")
    where = lax.axis_index("seq")
    model_width = x_big.shape[2]
    big_crops, big_length = (x_big.shape[0], x_big.shape[1])
    small_crops, small_length = (x_small.shape[0], x_small.shape[1])
    big_rows = big_crops * big_length
    mask_big = lax.dynamic_slice_in_dim(mask_big, where * big_crops, big_crops, 0)
    mask_small = lax.dynamic_slice_in_dim(mask_small, where * small_crops, small_crops, 0)
    qkv_full, gain_one, shift_one, bias_qv, bias_out, gain_two, shift_two, bias_up, bias_down = (
        gather_mats([w_qkv, ln1_gain, ln1_bias, b_qv, b_out, ln2_gain, ln2_bias, b_up, b_down])
    )
    out_full, up_full, down_full = gather_mats([w_out, w_up, w_down])
    gain_one, shift_one, bias_qv, bias_out, gain_two, shift_two, bias_up, bias_down = tuple(
        (
            vec.astype(jnp.float32)
            for vec in (
                gain_one,
                shift_one,
                bias_qv,
                bias_out,
                gain_two,
                shift_two,
                bias_up,
                bias_down,
            )
        )
    )
    tokens = jnp.concatenate(
        [x_big.reshape(big_rows, model_width), x_small.reshape(-1, model_width)], axis=0
    ).astype(jnp.float32)
    normed_one, pull_one = jax.vjp(layer_norm, tokens, gain_one, shift_one)
    input_one = normed_one.astype(jnp.bfloat16)
    bias_qkv = jnp.concatenate(
        [bias_qv[:model_width], jnp.zeros((model_width,), jnp.float32), bias_qv[model_width:]]
    )
    projected = (
        jnp.dot(input_one, qkv_full, preferred_element_type=jnp.float32) + bias_qkv
    ).astype(jnp.bfloat16)
    heads_big = projected[:big_rows].reshape(big_crops, big_length, -1)
    heads_small = projected[big_rows:].reshape(small_crops, small_length, -1)
    mixed_big, total_big = attend(heads_big, mask_big)
    mixed_small, total_small = attend(heads_small, mask_small)
    mixed_tok = jnp.concatenate([mixed_big, mixed_small], axis=0)
    middle = tokens + jnp.dot(mixed_tok, out_full, preferred_element_type=jnp.float32) + bias_out
    normed_two, pull_two = jax.vjp(layer_norm, middle, gain_two, shift_two)
    input_two = normed_two.astype(jnp.bfloat16)
    up_proj = jnp.dot(input_two, up_full, preferred_element_type=jnp.float32) + bias_up
    activated_f, pull_act = jax.vjp(gelu_exact, up_proj)
    activated = activated_f.astype(jnp.bfloat16)
    result = middle + jnp.dot(activated, down_full, preferred_element_type=jnp.float32) + bias_down
    grad_out = jnp.concatenate(
        [dy_big.reshape(big_rows, model_width), dy_small.reshape(-1, model_width)], axis=0
    )
    grad_down = jnp.einsum("ti,tj->ij", activated, grad_out, preferred_element_type=jnp.float32)
    grad_bias_down = jnp.sum(grad_out.astype(jnp.float32), axis=0)
    grad_act = jnp.einsum("tj,ij->ti", grad_out, down_full, preferred_element_type=jnp.float32)
    (grad_up_f,) = pull_act(grad_act)
    grad_up_b = grad_up_f.astype(jnp.bfloat16)
    grad_upw = jnp.einsum("ti,tj->ij", input_two, grad_up_b, preferred_element_type=jnp.float32)
    grad_bias_up = jnp.sum(grad_up_b.astype(jnp.float32), axis=0)
    grad_in_two = jnp.einsum("tj,ij->ti", grad_up_b, up_full, preferred_element_type=jnp.float32)
    grad_middle_ln, grad_gain_two, grad_shift_two = pull_two(grad_in_two)
    grad_middle = grad_out.astype(jnp.float32) + grad_middle_ln
    grad_branch = grad_middle.astype(jnp.bfloat16)
    grad_bias_out = jnp.sum(grad_branch.astype(jnp.float32), axis=0)
    grad_outw = jnp.einsum("ti,tj->ij", mixed_tok, grad_branch, preferred_element_type=jnp.float32)
    grad_mixed = jnp.einsum(
        "tj,ij->ti", grad_branch, out_full, preferred_element_type=jnp.float32
    ).astype(jnp.bfloat16)
    grad_projected = jnp.concatenate(
        [
            attend_back(heads_big, mask_big, total_big, grad_mixed[:big_rows]),
            attend_back(heads_small, mask_small, total_small, grad_mixed[big_rows:]),
        ],
        axis=0,
    )
    grad_qkvw = jnp.einsum(
        "ti,tj->ij", input_one, grad_projected, preferred_element_type=jnp.float32
    )
    grad_proj_sums = jnp.sum(grad_projected.astype(jnp.float32), axis=0)
    grad_bias_qv = jnp.concatenate(
        [grad_proj_sums[:model_width], grad_proj_sums[2 * model_width :]]
    )
    grad_in_one = jnp.einsum(
        "tj,ij->ti", grad_projected, qkv_full, preferred_element_type=jnp.float32
    )
    grad_tokens_ln, grad_gain_one, grad_shift_one = pull_one(grad_in_one)
    grad_tokens = (grad_middle + grad_tokens_ln).astype(jnp.bfloat16)
    vectors = (
        grad_gain_one,
        grad_shift_one,
        grad_bias_qv,
        grad_bias_out,
        grad_gain_two,
        grad_shift_two,
        grad_bias_up,
        grad_bias_down,
    )
    vector_sums = lax.psum(jnp.concatenate(vectors), AXES)
    vec_out, at = ([], 0)
    for v in vectors:
        width = v.shape[0] // n_seq
        vec_out.append(lax.dynamic_slice(vector_sums, (at + where * width,), (width,)))
        at += v.shape[0]
    g_up, g_down = scatter_mats([grad_upw, grad_down])
    g_qkv, g_out = scatter_mats([grad_qkvw, grad_outw])
    y_big = result[:big_rows].reshape(big_crops, big_length, model_width).astype(jnp.bfloat16)
    y_small = result[big_rows:].reshape(small_crops, small_length, model_width).astype(jnp.bfloat16)
    dx_big = grad_tokens[:big_rows].reshape(big_crops, big_length, model_width)
    dx_small = grad_tokens[big_rows:].reshape(small_crops, small_length, model_width)
    return (
        y_big,
        y_small,
        dx_big,
        dx_small,
        vec_out[0],
        vec_out[1],
        g_qkv,
        vec_out[2],
        g_out,
        vec_out[3],
        vec_out[4],
        vec_out[5],
        g_up,
        vec_out[6],
        g_down,
        vec_out[7],
    )


def solution(mesh):
    rows3 = P(AXES, None, None)
    placed = (
        rows3,
        rows3,
        P("img", None),
        P("img", None),
        P("seq"),
        P("seq"),
        P("img", "seq"),
        P("seq"),
        P("img", "seq"),
        P("seq"),
        P("seq"),
        P("seq"),
        P("img", "seq"),
        P("seq"),
        P("img", "seq"),
        P("seq"),
        rows3,
        rows3,
    )
    return jax.shard_map(
        body,
        mesh=mesh,
        in_specs=placed,
        out_specs=(rows3,) * 4
        + (
            P("seq"),
            P("seq"),
            P("img", "seq"),
            P("seq"),
            P("img", "seq"),
            P("seq"),
            P("seq"),
            P("seq"),
            P("img", "seq"),
            P("seq"),
            P("img", "seq"),
            P("seq"),
        ),
        check_vma=False,
    )
```

profile of v0, /device:TPU:0, one launch (start us, length us, event | category | flops | bytes accessed | tf_op | source)
XLA Modules:
  0.0 870.6 jit_solution(1051177203787296150)
XLA Ops:
  25.0 55.9 %all-gather.7.cloned.1.call-done = bf16[32,900,64]{1,2,0:T(8,128)(2,1)} async-done(((bf16[1,900,64]{1,2,0:T(8,128)(2,1)}), bf16[32,900,64]{1,2,0:T(8,128)(2,1)}) %all-gather.7.cloned.1.call-update) | async-done | bytes 3686416 | tf_op jit(solution)/shard_map/all_gather | solution.py:76
  88.9 8.3 copy.143
  97.2 10.8 %reshape.350 = bf16[8,4,96,576]{3,2,1,0:T(8,128)(2,1)} reshape(bf16[32,864,64]{2,1,0:T(8,128)(2,1)} %copy.143) | data formatting | bytes 7077888 | tf_op jit(solution)/shard_map/reshape | solution.py:80
  108.0 6.1 copy.144
  114.1 7.8 reshape.351
  122.0 9.1 %fusion.8 = bf16[1440,2304]{1,0:T(8,128)(2,1)S(1)} fusion(bf16[768,2304]{1,0:T(8,128)(2,1)} %reshape.351, f32[2304]{0:T(1024)S(1)} %pad_maximum_fusion.12, f32[768]{0:T(1024)S(1)} %reshape.378, f32[768]{0:T(1024)S(1)} %reshape.377, f32[1440]{0:T(1024)S(1)} %fusion.103, f32[1440]{0:T(1024)S(1)} %broadcast_multiply_fusion.1, ...), kind=kOutput, calls=%fused_computation.22 | convolution fusion | flops 5112668160 | bytes 12413184 | tf_op jit(solution)/shard_map/dot_general | solution.py:163
  136.7 9.8 %reshape_reshape.9 = bf16[16,40,3,12,64]{4,3,2,1,0:T(8,128)(2,1)} reshape(bf16[640,2304]{1,0:T(8,128)(2,1)} %slice.190) | data formatting | bytes 5898240 | tf_op jit(solution)/shard_map/reshape;reshape | solution.py:26
  162.9 5.6 reshape.396
  168.5 12.1 %reshape.398 = bf16[4,200,3,12,64]{4,3,2,1,0:T(8,128)(2,1)} reshape(bf16[800,2304]{1,0:T(8,128)(2,1)} %slice.186) | data formatting | bytes 7372800 | tf_op jit(solution)/shard_map/reshape;reshape | solution.py:26
  180.5 7.0 fusion.136
  239.9 14.1 %fusion.135 = (bf16[32,1152,64]{1,2,0:T(8,128)(2,1)}, bf16[32,1152,64]{1,2,0:T(8,128)(2,1)}) fusion(bf16[32,2592,64]{1,2,0:T(8,128)(2,1)} %all-gather.9.cloned.1.call-done), kind=kLoop, calls=%fused_computation.187 | loop fusion | bytes 18874368 | tf_op jit(solution)/shard_map/slice | solution.py:80
  254.0 9.6 %copy.174 = bf16[32,1152,64]{2,1,0:T(8,128)(2,1)} copy(bf16[32,1152,64]{1,2,0:T(8,128)(2,1)} %get-tuple-element.77) | data formatting | bytes 9437184 | tf_op jit(solution)/shard_map/slice | solution.py:80
  263.7 15.5 %reshape.361 = bf16[8,4,384,192]{3,2,1,0:T(8,128)(2,1)} reshape(bf16[32,1152,64]{2,1,0:T(8,128)(2,1)} %copy.174) | data formatting | bytes 9437184 | tf_op jit(solution)/shard_map/reshape | solution.py:80
  279.2 8.8 %copy.175 = bf16[8,384,4,192]{1,0,3,2:T(8,128)(2,1)} copy(bf16[8,384,4,192]{3,1,2,0:T(8,128)(2,1)} %bitcast.150) | data formatting | bytes 9437184 | tf_op jit(solution)/shard_map/transpose | solution.py:83
  288.0 5.7 copy.225
  293.6 9.6 %copy.170 = bf16[32,1152,64]{2,1,0:T(8,128)(2,1)} copy(bf16[32,1152,64]{1,2,0:T(8,128)(2,1)} %get-tuple-element.78) | data formatting | bytes 9437184 | tf_op jit(solution)/shard_map/slice | solution.py:80
  303.3 13.4 %reshape.359 = bf16[8,4,96,768]{3,2,1,0:T(8,128)(2,1)} reshape(bf16[32,1152,64]{2,1,0:T(8,128)(2,1)} %copy.170) | data formatting | bytes 9437184 | tf_op jit(solution)/shard_map/reshape | solution.py:80
  316.6 6.0 copy.171
  328.1 48.1 %multiply_convert_fusion = (bf16[1440,3072]{1,0:T(8,128)(2,1)}, f32[1440,3072]{1,0:T(8,128)}, f32[1440,3072]{1,0:T(8,128)}) fusion(f32[3072]{0:T(1024)S(1)} %reshape.382, bf16[768,3072]{1,0:T(8,128)(2,1)S(1)} %bitcast.185, f32[1440,768]{1,0:T(8,128)S(1)} %get-tuple-element.108, f32[768]{0:T(1024)S(1)} %reshape.381, f32[768]{0:T(1024)S(1)} %reshape.380, ...), kind=kOutput, calls=%fused_computation.6 | convolution fusion | flops 7092264960 | bytes 53409024 | tf_op jit(solution)/shard_map/dot_general | solution.py:173
  376.3 21.3 %convert_reduce_fusion = (f32[3072]{0:T(1024)}, bf16[1440,3072]{1,0:T(8,128)(2,1)}) fusion(f32[1440,3072]{1,0:T(8,128)} %get-tuple-element.76, bf16[3072,768]{0,1:T(8,128)(2,1)S(1)} %bitcast.184, bf16[640,768]{1,0:T(8,128)(2,1)} %bitcast.187, bf16[800,768]{1,0:T(8,128)(2,1)S(1)} %bitcast.177, f32[1440,3072]{1,0:T(8,128)} %get-tuple-element.109, ...), kind=kOutput, calls=%fused_computation.4 | convolution fusion | flops 6874395648 | bytes 51191808 | tf_op jit(solution)/shard_map/tj,ij->ti/dot_general | solution.py:182
  397.6 13.7 %multiply_reduce_fusion.1 = (f32[768]{0:T(1024)}, f32[1440]{0:T(1024)S(1)}, f32[768]{0:T(1024)}, f32[1440,768]{1,0:T(8,128)S(1)}) fusion(f32[1440,768]{1,0:T(8,128)S(1)} %get-tuple-element.108, f32[1440]{0:T(1024)S(1)} %fusion.104, f32[1440]{0:T(1024)S(1)} %broadcast_multiply_fusion, f32[768]{0:T(1024)S(1)} %reshape.380, ...), kind=kOutput, calls=%fused_computation.67 | convolution fusion | flops 6803616768 | bytes 22439808 | tf_op jit(solution)/shard_map/tj,ij->ti/dot_general | solution.py:187
  434.6 10.0 %convert_bitcast_fusion.2 = bf16[16,40,1,12,64]{4,1,3,0,2:T(8,128)(2,1)} fusion(f32[16,12,40,40]{2,3,1,0:T(8,128)} %fusion.100, f32[16,12,40,40]{2,3,1,0:T(8,128)} %copy-done.8, f32[16,12,40]{2,1,0:T(8,128)S(1)} %copy-done.35, bf16[16,40,1,12,64]{4,3,2,1,0:T(8,128)(2,1)} %copy-done.26), kind=kOutput, calls=%fused_computation.98 | convolution fusion | flops 41971240 | bytes 4454400 | tf_op jit(solution)/shard_map/chqk,ckhd->cqhd/dot_general | solution.py:59
  444.6 9.2 %convert_bitcast_fusion.1 = bf16[16,40,1,12,64]{4,1,3,0,2:T(8,128)(2,1)} fusion(f32[16,12,40,40]{2,3,1,0:T(8,128)} %fusion.100, f32[16,12,40,40]{2,3,1,0:T(8,128)} %copy-done.8, f32[16,12,40]{2,1,0:T(8,128)S(1)} %copy-done.35, bf16[16,40,1,12,64]{4,3,2,1,0:T(8,128)(2,1)S(1)} %copy-done.25), kind=kOutput, calls=%fused_computation.97 | convolution fusion | flops 41971240 | bytes 4454400 | tf_op jit(solution)/shard_map/chqk,cqhd->ckhd/dot_general | solution.py:62
  460.9 7.3 fusion.81
  468.2 7.3 fusion.97
  475.5 19.7 %fusion.92 = bf16[4,200,1,12,64]{1,4,3,0,2:T(8,128)(2,1)} fusion(f32[4,12,200,200]{2,3,1,0:T(8,128)} %fusion.81, f32[4,12,200]{2,1,0:T(8,128)S(1)} %copy-done.46, f32[4,12,200,200]{2,3,1,0:T(8,128)} %copy-done.3, pred[4,200]{1,0:T(4,128)(4,1)S(1)} %copy-done.52, bf16[4,200,1,12,64]{1,4,3,0,2:T(8,128)(2,1)S(1)} %copy-done.17), kind=kOutput, calls=%fused_computation.122 | convolution fusion | flops 267504192 | bytes 17856800 | tf_op jit(solution)/shard_map/chqk,ckhd->cqhd/dot_general | solution.py:59
  495.2 19.0 %fusion.87 = bf16[4,200,1,12,64]{1,4,3,0,2:T(8,128)(2,1)} fusion(f32[4,12,200,200]{2,3,1,0:T(8,128)} %fusion.81, f32[4,12,200]{2,1,0:T(8,128)S(1)} %copy-done.46, f32[4,12,200,200]{2,3,1,0:T(8,128)} %copy-done.3, pred[4,200]{1,0:T(4,128)(4,1)S(1)} %copy-done.52, bf16[4,200,1,12,64]{1,4,3,0,2:T(8,128)(2,1)S(1)} %copy-done.15), kind=kOutput, calls=%fused_computation.121 | convolution fusion | flops 267504192 | bytes 17856800 | tf_op jit(solution)/shard_map/chqk,cqhd->ckhd/dot_general | solution.py:62
  522.7 5.9 pad_maximum_fusion.2
  528.6 12.8 %copy.203 = bf16[16,40,3,12,64]{1,0,4,3,2:T(8,128)(2,1)} copy(bf16[16,40,3,12,64]{4,1,3,0,2:T(8,128)(2,1)} %pad_maximum_fusion.2) | data formatting | bytes 5898240 | tf_op jit(solution)/shard_map/convert_element_type | solution.py:69
  541.3 14.1 %reshape.397 = bf16[640,2304]{0,1:T(8,128)(2,1)} reshape(bf16[16,40,3,12,64]{1,0,4,3,2:T(8,128)(2,1)} %copy.203) | data formatting | bytes 5898240 | tf_op jit(solution)/shard_map/convert_element_type | solution.py:69
  558.1 6.6 copy.184
  564.8 9.7 %convert_element_type.280 = bf16[800,2304]{0,1:T(8,128)(2,1)} reshape(bf16[4,200,3,12,64]{1,0,4,3,2:T(4,128)(2,1)} %copy.184) | data formatting | bytes 7372800 | tf_op jit(solution)/shard_map/convert_element_type | solution.py:69
  574.5 12.6 %convolution_convert_fusion = bf16[768,2304]{1,0:T(8,128)(2,1)} fusion(bf16[640,2304]{0,1:T(8,128)(2,1)} %reshape.397, bf16[800,2304]{0,1:T(8,128)(2,1)} %convert_element_type.280, f32[768]{0:T(1024)S(1)} %copy-done.54, f32[768]{0:T(1024)S(1)} %copy-done.48, f32[1440]{0:T(1024)S(1)} %copy-done.39, f32[1440]{0:T(1024)S(1)} %copy-done.37, ...), kind=kOutput, calls=%fused_computation.48 | convolution fusion | flops 5121073152 | bytes 12403968 | tf_op jit(solution)/shard_map/ti,tj->ij/dot_general | solution.py:203
  587.1 9.1 %reshape.369 = bf16[8,96,4,576]{3,2,1,0:T(4,128)(2,1)} reshape(bf16[768,2304]{1,0:T(8,128)(2,1)} %convolution_convert_fusion) | data formatting | bytes 7077888 | tf_op jit(solution)/shard_map/reshape | solution.py:95
  600.8 7.9 reshape.370
  614.8 12.5 %convolution_convert_fusion.1 = bf16[3072,768]{1,0:T(8,128)(2,1)} fusion(bf16[1440,3072]{1,0:T(8,128)(2,1)} %get-tuple-element.75, bf16[640,768]{1,0:T(8,128)(2,1)} %bitcast.188, bf16[800,768]{1,0:T(8,128)(2,1)S(1)} %bitcast.179), kind=kOutput, calls=%fused_computation.49 | convolution fusion | flops 6801555456 | bytes 15777792 | tf_op jit(solution)/shard_map/ti,tj->ij/dot_general | solution.py:180
  627.3 6.7 copy.193
  634.0 5.8 copy.226
  639.7 14.1 %convolution_convert_fusion.2 = bf16[768,3072]{1,0:T(8,128)(2,1)} fusion(bf16[1440,3072]{1,0:T(8,128)(2,1)} %get-tuple-element.113, f32[1440,768]{1,0:T(8,128)} %copy-done.6, f32[768]{0:T(1024)S(1)} %copy-done.56, f32[768]{0:T(1024)S(1)} %reshape.380, f32[1440]{0:T(1024)S(1)} %fusion.104, f32[1440]{0:T(1024)S(1)} %broadcast_multiply_fusion), kind=kOutput, calls=%fused_computation.50 | convolution fusion | flops 6802661376 | bytes 18007296 | tf_op jit(solution)/shard_map/ti,tj->ij/dot_general | solution.py:185
  653.8 9.8 %reshape.373 = bf16[8,96,4,768]{3,2,1,0:T(4,128)(2,1)} reshape(bf16[768,3072]{1,0:T(8,128)(2,1)} %convolution_convert_fusion.2) | data formatting | bytes 9437184 | tf_op jit(solution)/shard_map/reshape | solution.py:95
  669.0 9.3 %reshape.374 = bf16[32,576,128]{2,1,0:T(8,128)(2,1)} reshape(bf16[8,4,96,768]{3,2,1,0:T(8,128)(2,1)} %bitcast.162) | data formatting | bytes 9437184 | tf_op jit(solution)/shard_map/reshape | solution.py:96
  678.3 9.3 %copy.194 = bf16[8,4,384,192]{3,2,1,0:T(8,128)(2,1)} copy(bf16[8,4,384,192]{2,0,3,1:T(8,128)(2,1)} %bitcast.163) | data formatting | bytes 9437184 | tf_op jit(solution)/shard_map/transpose | solution.py:95
  687.6 12.0 %reshape.376 = bf16[32,576,128]{2,1,0:T(8,128)(2,1)} reshape(bf16[8,4,384,192]{3,2,1,0:T(8,128)(2,1)} %copy.194) | data formatting | bytes 9437184 | tf_op jit(solution)/shard_map/reshape | solution.py:96
  699.6 7.7 pad_maximum_fusion
  708.4 13.1 %add_convert_fusion.2 = bf16[1440,768]{1,0:T(8,128)(2,1)S(1)} fusion(f32[1440,768]{1,0:T(8,128)} %copy-done.6, bf16[1440,3072]{1,0:T(8,128)(2,1)} %get-tuple-element.75, bf16[3072,768]{0,1:T(8,128)(2,1)} %bitcast.181, f32[768]{0:T(1024)S(1)} %reshape.383), kind=kOutput, calls=%fused_computation.71 | convolution fusion | flops 6798090240 | bytes 20204544 | tf_op jit(solution)/shard_map/dot_general | solution.py:176
  723.6 11.4 %fusion.131 = (f32[768]{0:T(1024)S(1)}, f32[1440]{0:T(1024)S(1)}, f32[1440,768]{1,0:T(8,128)S(1)}) fusion(f32[768]{0:T(1024)S(1)} %copy-done.48, f32[1440]{0:T(1024)S(1)} %copy-done.37, bf16[640,768]{1,0:T(8,128)(2,1)S(1)} %bitcast.172, bf16[800,768]{1,0:T(8,128)(2,1)S(1)} %bitcast.156, bf16[768,2304]{1,0:T(8,128)(2,1)} %reshape.351, ...), kind=kOutput, calls=%fused_computation.185 | convolution fusion | flops 5119301120 | bytes 16827648 | tf_op jit(solution)/shard_map/tj,ij->ti/dot_general | solution.py:210
  749.7 39.8 %psum.7 = f32[9216]{0:T(1024)S(1)} all-reduce(f32[9216]{0:T(1024)S(1)} %constant_dynamic-update-slice_fusion), channel_id=1, replica_groups=mesh['img'=8,'seq'=4] {'img','seq'}, use_global_device_ids=true, to_apply=%region_22.23 | all-reduce | flops 9216 | bytes 73728 | tf_op jit(solution)/shard_map/psum | solution.py:225
  794.7 66.3 %reduce-scatter.5.cloned.1.call-done = bf16[1,1152,128]{2,1,0:T(8,128)(2,1)} async-done(((bf16[32,1152,128]{2,1,0:T(8,128)(2,1)}), bf16[1,1152,128]{2,1,0:T(8,128)(2,1)}) %reduce-scatter.5.cloned.1.call-update) | async-done | bytes 294928 | tf_op jit(solution)/shard_map/reduce_scatter | solution.py:98
  (277 shorter events, 188.3 us)
Async XLA Ops:
  7.2 15.2 %copy-start = (s32[64,40]{0,1:T(8,128)S(1)}, s32[64,40]{0,1:T(8,128)}, u32[]{:S(2)}) copy-start(s32[64,40]{0,1:T(8,128)} %param.21) | copy-start | bytes 30724
  7.2 15.3 %copy-start.10 = (bf16[16,40,768]{2,1,0:T(8,128)(2,1)S(1)}, bf16[16,40,768]{2,1,0:T(8,128)(2,1)}, u32[]{:S(2)}) copy-start(bf16[16,40,768]{2,1,0:T(8,128)(2,1)} %param.19) | copy-start | bytes 2949124
  7.2 15.3 %copy-start.4 = (bf16[4,200,768]{2,1,0:T(8,128)(2,1)S(1)}, bf16[4,200,768]{2,1,0:T(8,128)(2,1)}, u32[]{:S(2)}) copy-start(bf16[4,200,768]{2,1,0:T(8,128)(2,1)} %param.18) | copy-start | bytes 3686404
  7.2 73.8 %all-gather.7.cloned.1.call-start = ((), (), s32[]{:S(2)}) async-start(), calls=%async_computation.4 | async-start | bytes 4325376 | tf_op jit(solution)/shard_map/all_gather | solution.py:76
  16.0 205.4 %all-gather.9.cloned.1.call-start = ((), (), s32[]{:S(2)}) async-start(), calls=%async_computation.5 | async-start | bytes 11354112 | tf_op jit(solution)/shard_map/all_gather | solution.py:76
  22.3 769.2 %reduce-scatter.3.cloned.1.call-start = ((), (), s32[]{:S(2)}) async-start(), calls=%async_computation.2 | async-start | bytes 4866048 | tf_op jit(solution)/shard_map/reduce_scatter | solution.py:98
  23.6 185.4 %copy-start.51 = (pred[4,200]{1,0:T(4,128)(4,1)}, pred[4,200]{1,0:T(4,128)(4,1)S(1)}, u32[]{:S(2)}) copy-start(pred[4,200]{1,0:T(4,128)(4,1)S(1)} %dynamic-slice_compare_fusion) | copy-start | bytes 2404
  23.6 98.3 %copy-start.36 = (f32[1440]{0:T(1024)}, f32[1440]{0:T(1024)S(1)}, u32[]{:S(2)}) copy-start(f32[1440]{0:T(1024)S(1)} %broadcast_multiply_fusion.1) | copy-start | bytes 17284
  25.0 96.9 %copy-start.38 = (f32[1440]{0:T(1024)}, f32[1440]{0:T(1024)S(1)}, u32[]{:S(2)}) copy-start(f32[1440]{0:T(1024)S(1)} %fusion.103) | copy-start | bytes 17284
  84.5 37.5 %copy-start.53 = (f32[768]{0:T(1024)}, f32[768]{0:T(1024)S(1)}, u32[]{:S(2)}) copy-start(f32[768]{0:T(1024)S(1)} %reshape.378) | copy-start | bytes 9220
  84.7 37.3 %copy-start.47 = (f32[768]{0:T(1024)}, f32[768]{0:T(1024)S(1)}, u32[]{:S(2)}) copy-start(f32[768]{0:T(1024)S(1)} %reshape.377) | copy-start | bytes 9220
  136.4 191.7 %copy-start.55 = (f32[768]{0:T(1024)}, f32[768]{0:T(1024)S(1)}, u32[]{:S(2)}) copy-start(f32[768]{0:T(1024)S(1)} %reshape.381) | copy-start | bytes 9220
  324.6 51.7 %slice-start.2 = ((s8[4718592]{0:T(1024)(128)(4,1)}), s8[524288]{0:T(1024)(128)(4,1)S(1)}, s32[]{:S(2)}) async-start(s8[4718592]{0:T(1024)(128)(4,1)} %bitcast.182), calls=%async_computation.8 | async-start | bytes 1048576
  327.4 83.9 %copy-start.6 = (f32[1440,768]{1,0:T(8,128)}, f32[1440,768]{1,0:T(8,128)S(1)}, u32[]{:S(2)}) copy-start(f32[1440,768]{1,0:T(8,128)S(1)} %get-tuple-element.108) | copy-start | bytes 13271044
  328.1 48.2 %copy-start.44 = (f32[1440]{0:T(1024)}, f32[1440]{0:T(1024)S(1)}, u32[]{:S(2)}) copy-start(f32[1440]{0:T(1024)S(1)} %multiply_reduce_fusion.3) | copy-start | bytes 17284
  328.1 48.2 %copy-start.19 = (bf16[4,200,768]{2,1,0:T(8,128)(2,1)S(1)}, bf16[4,200,768]{2,1,0:T(8,128)(2,1)}, u32[]{:S(2)}) copy-start(bf16[4,200,768]{2,1,0:T(8,128)(2,1)} %param.34) | copy-start | bytes 3686404
  328.1 48.2 %slice-start.3 = ((s8[4718592]{0:T(1024)(128)(4,1)}), s8[4194304]{0:T(1024)(128)(4,1)S(1)}, s32[]{:S(2)}) async-start(s8[4718592]{0:T(1024)(128)(4,1)} %bitcast.182), calls=%async_computation.9 | async-start | bytes 8388608
  397.6 13.7 %copy-start.45 = (f32[1440]{0:T(1024)S(1)}, f32[1440]{0:T(1024)}, u32[]{:S(2)}) copy-start(f32[1440]{0:T(1024)} %copy-done.44) | copy-start | bytes 17284
  427.1 5.0 copy-start.9
  427.2 5.0 copy-start.35
  434.6 10.1 %copy-start.25 = (bf16[16,40,1,12,64]{4,3,2,1,0:T(8,128)(2,1)S(1)}, bf16[16,40,1,12,64]{4,3,2,1,0:T(8,128)(2,1)}, u32[]{:S(2)}) copy-start(bf16[16,40,1,12,64]{4,3,2,1,0:T(8,128)(2,1)} %copy-done.24) | copy-start | bytes 2949124
  460.9 7.3 copy-start.18
  460.9 7.3 copy-start.46
  460.9 7.3 copy-start.52
  468.2 7.3 copy-start.17
  475.5 19.7 %copy-start.15 = (bf16[4,200,1,12,64]{1,4,3,0,2:T(8,128)(2,1)S(1)}, bf16[4,200,1,12,64]{1,4,3,0,2:T(8,128)(2,1)}, u32[]{:S(2)}) copy-start(bf16[4,200,1,12,64]{1,4,3,0,2:T(8,128)(2,1)} %copy.213) | copy-start | bytes 3686404
  495.2 19.0 %copy-start.32 = (bf16[768,768]{1,0:T(8,128)(2,1)S(1)}, bf16[768,768]{1,0:T(8,128)(2,1)}, u32[]{:S(2)}) copy-start(bf16[768,768]{1,0:T(8,128)(2,1)} %convolution_convert_fusion.4) | copy-start | bytes 3538948
  514.2 8.5 copy-start.14
  541.3 14.1 %copy-start.27 = (bf16[4,200,1,12,64]{1,4,3,0,2:T(8,128)(2,1)S(1)}, bf16[4,200,1,12,64]{1,4,3,0,2:T(8,128)(2,1)}, u32[]{:S(2)}) copy-start(bf16[4,200,1,12,64]{1,4,3,0,2:T(8,128)(2,1)} %fusion.97) | copy-start | bytes 3686404
  564.7 9.8 %copy-start.5 = (bf16[4,200,768]{2,1,0:T(8,128)(2,1)S(1)}, bf16[4,200,768]{2,1,0:T(8,128)(2,1)}, u32[]{:S(2)}) copy-start(bf16[4,200,768]{2,1,0:T(8,128)(2,1)} %param.18) | copy-start | bytes 3686404
  564.7 9.8 %copy-start.11 = (bf16[16,40,768]{2,1,0:T(8,128)(2,1)S(1)}, bf16[16,40,768]{2,1,0:T(8,128)(2,1)}, u32[]{:S(2)}) copy-start(bf16[16,40,768]{2,1,0:T(8,128)(2,1)} %param.19) | copy-start | bytes 2949124
  564.7 9.8 %copy-start.37 = (f32[1440]{0:T(1024)S(1)}, f32[1440]{0:T(1024)}, u32[]{:S(2)}) copy-start(f32[1440]{0:T(1024)} %copy-done.36) | copy-start | bytes 17284
  564.7 9.8 %copy-start.39 = (f32[1440]{0:T(1024)S(1)}, f32[1440]{0:T(1024)}, u32[]{:S(2)}) copy-start(f32[1440]{0:T(1024)} %copy-done.38) | copy-start | bytes 17284
  564.7 9.8 %copy-start.48 = (f32[768]{0:T(1024)S(1)}, f32[768]{0:T(1024)}, u32[]{:S(2)}) copy-start(f32[768]{0:T(1024)} %copy-done.47) | copy-start | bytes 9220
  564.8 9.8 %copy-start.54 = (f32[768]{0:T(1024)S(1)}, f32[768]{0:T(1024)}, u32[]{:S(2)}) copy-start(f32[768]{0:T(1024)} %copy-done.53) | copy-start | bytes 9220
  613.6 247.5 %reduce-scatter.5.cloned.1.call-start = ((), (), s32[]{:S(2)}) async-start(), calls=%async_computation.3 | async-start | bytes 9732096 | tf_op jit(solution)/shard_map/reduce_scatter | solution.py:98
  634.0 5.8 copy-start.56
  708.4 15.2 %copy-start.7 = (bf16[800,2304]{0,1:T(8,128)(2,1)S(1)}, bf16[800,2304]{0,1:T(8,128)(2,1)}, u32[]{:S(2)}) copy-start(bf16[800,2304]{0,1:T(8,128)(2,1)} %convert_element_type.280) | copy-start | bytes 11059204
  722.5 16.6 %slice-start = ((s8[4423680]{0:T(1024)(128)(4,1)}), s8[4194304]{0:T(1024)(128)(4,1)S(1)}, s32[]{:S(2)}) async-start(s8[4423680]{0:T(1024)(128)(4,1)} %bitcast.148), calls=%async_computation.6 | async-start | bytes 8388608
  723.6 11.4 %copy-start.43 = (f32[1440]{0:T(1024)S(1)}, f32[1440]{0:T(1024)}, u32[]{:S(2)}) copy-start(f32[1440]{0:T(1024)} %copy-done.42) | copy-start | bytes 17284
  723.6 15.5 %slice-start.1 = ((s8[4423680]{0:T(1024)(128)(4,1)}), s8[229376]{0:T(1024)(128)(4,1)S(1)}, s32[]{:S(2)}) async-start(s8[4423680]{0:T(1024)(128)(4,1)} %bitcast.148), calls=%async_computation.7 | async-start | bytes 458752
  735.0 4.1 copy-start.23
  735.0 4.1 copy-start.41
  744.2 5.4 copy-start.49
  744.2 5.4 copy-start.58
  744.2 5.4 copy-start.57
  744.2 5.5 copy-start.50
  745.3 118.5 %copy-start.1 = (s32[64,40]{0,1:T(8,128)S(1)}, s32[64,40]{0,1:T(8,128)}, u32[]{:S(2)}) copy-start(s32[64,40]{0,1:T(8,128)} %param.21) | copy-start | bytes 30724
  (19 other events, 46.9 us)
Sparse Core Ops, SparseCore 0:
  16.2 64.7 all-gather.6
  84.4 87.4 all-gather.8
  613.7 105.7 reduce-scatter.2
  726.2 134.7 reduce-scatter.4
where the time goes:
time: 880 us; the launch traced here: 871 us
  local copies, waits for them, and re-layouts  376 us (43%)
  matrix products  256 us (29%)
  waiting for transfers between devices  122 us (14%)
  other arithmetic  62.1 us (7%)
  blocking collectives  39.8 us (5%)
  between operations  14.9 us (2%)
    reduce_scatter x2, waiting for transfers between devices, scatter_mats(): mine = lax.psum_scatter(flat, AXES, scatter_dimension=0, tiled=False)  66.3 us
    all_gather x2, waiting for transfers between devices, gather_mats(): whole = lax.all_gather(flat, AXES, axis=0, tiled=False)  55.9 us
    slice x7, local copies, waits for them, and re-layouts, gather_mats(): piece = whole[:, at:at + rows].reshape((n_img, n_seq) + m.shape)  52.6 us
    dot_general x1, matrix products, body(): jnp.dot(input_two, up_full, preferred_element_type=jnp.float32) + bias_up  48.1 us
    reshape x4, local copies, waits for them, and re-layouts, gather_mats(): piece = whole[:, at:at + rows].reshape((n_img, n_seq) + m.shape)  44.4 us
    psum x1, blocking collectives, body(): vector_sums = lax.psum(jnp.concatenate(vectors), AXES)  39.8 us
    unnamed x144, local copies, waits for them, and re-layouts  36.7 us
    convert_element_type x3, local copies, waits for them, and re-layouts, attend_back(): jnp.stack([grad_query, grad_key, grad_value], axis=2).astype(jnp.bfloat16)  36.6 us
  transfers between devices with their start and end apart: 4, of which 2 were waited for; matrix products, arithmetic and copies ran while one was open for 33% of the time, Pallas kernels for 0%

commit v1 on v0

--- a/solution.py
+++ b/solution.py
@@ -222,7 +222,7 @@
         grad_bias_up,
         grad_bias_down,
     )
-    vector_sums = lax.psum(jnp.concatenate(vectors), AXES)
+    vector_sums = jnp.sum(lax.all_gather(jnp.concatenate(vectors), AXES), axis=0)
     vec_out, at = ([], 0)
     for v in vectors:
         width = v.shape[0] // n_seq

time: 880 us -> 917 us (1.042)
  waiting for transfers between devices: 122 us -> 186 us
  blocking collectives: 39.8 us -> 0 us
    reduce_scatter x2, waiting for transfers between devices: 66.3 us -> 130 us  [scatter_mats(): mine = lax.psum_scatter(flat, AXES, scatter_dimension=0, tiled=False)]
    psum x1 -> x0, blocking collectives: 39.8 us -> none  [body(): vector_sums = lax.psum(jnp.concatenate(vectors), AXES)]
    unnamed x144 -> x142, local copies, waits for them, and re-layouts: 36.7 us -> 36.8 us
  transfers between devices with their start and end apart: 4 -> 5, of which waited for: 2 -> 2; matrix products, arithmetic and copies ran while one was open for 33% -> 35% of each run, Pallas kernels for 0% -> 0%
where the time goes in v1:
time: 917 us; the launch traced here: 907 us
  local copies, waits for them, and re-layouts  379 us (41%)
  matrix products  261 us (28%)
  waiting for transfers between devices  186 us (20%)
  other arithmetic  65.1 us (7%)
  between operations  15 us (2%)
    reduce_scatter x2, waiting for transfers between devices, scatter_mats(): mine = lax.psum_scatter(flat, AXES, scatter_dimension=0, tiled=False)  130 us
    all_gather x2, waiting for transfers between devices, gather_mats(): whole = lax.all_gather(flat, AXES, axis=0, tiled=False)  55.9 us
    slice x7, local copies, waits for them, and re-layouts, gather_mats(): piece = whole[:, at:at + rows].reshape((n_img, n_seq) + m.shape)  52.4 us
    dot_general x1, matrix products, body(): jnp.dot(input_two, up_full, preferred_element_type=jnp.float32) + bias_up  48.3 us
    reshape x4, local copies, waits for them, and re-layouts, gather_mats(): piece = whole[:, at:at + rows].reshape((n_img, n_seq) + m.shape)  44.5 us
    unnamed x142, local copies, waits for them, and re-layouts  36.8 us
    reshape x6, local copies, waits for them, and re-layouts, scatter_mats(): m.astype(jnp.bfloat16).reshape(n_img, rows, n_seq, cols)  36.5 us
    convert_element_type x3, local copies, waits for them, and re-layouts, attend_back(): jnp.stack([grad_query, grad_key, grad_value], axis=2).astype(jnp.bfloat16)  36.4 us
  transfers between devices with their start and end apart: 5, of which 2 were waited for; matrix products, arithmetic and copies ran while one was open for 35% of the time, Pallas kernels for 0%

profile of v1, /device:TPU:0, one launch (start us, length us, event | category | flops | bytes accessed | tf_op | source)
XLA Modules:
  0.0 906.9 jit_solution(3664651061660328891)
XLA Ops:
  25.1 55.9 %all-gather.11.cloned.1.call-done = bf16[32,900,64]{1,2,0:T(8,128)(2,1)} async-done(((bf16[1,900,64]{1,2,0:T(8,128)(2,1)}), bf16[32,900,64]{1,2,0:T(8,128)(2,1)}) %all-gather.11.cloned.1.call-update) | async-done | bytes 3686416 | tf_op jit(solution)/shard_map/all_gather | solution.py:76
  88.9 8.0 copy.194
  96.9 10.8 %reshape.350 = bf16[8,4,96,576]{3,2,1,0:T(8,128)(2,1)} reshape(bf16[32,864,64]{2,1,0:T(8,128)(2,1)} %copy.194) | data formatting | bytes 7077888 | tf_op jit(solution)/shard_map/reshape | solution.py:80
  107.7 6.1 copy.195
  113.8 7.8 reshape.351
  121.7 9.1 %fusion.8 = bf16[1440,2304]{1,0:T(8,128)(2,1)S(1)} fusion(bf16[768,2304]{1,0:T(8,128)(2,1)} %reshape.351, f32[2304]{0:T(1024)S(1)} %pad_maximum_fusion.12, f32[768]{0:T(1024)S(1)} %reshape.378, f32[768]{0:T(1024)S(1)} %reshape.377, f32[1440]{0:T(1024)S(1)} %fusion.103, f32[1440]{0:T(1024)S(1)} %broadcast_multiply_fusion.1, ...), kind=kOutput, calls=%fused_computation.22 | convolution fusion | flops 5112668160 | bytes 12413184 | tf_op jit(solution)/shard_map/dot_general | solution.py:163
  136.4 9.8 %reshape_reshape.9 = bf16[16,40,3,12,64]{4,3,2,1,0:T(8,128)(2,1)} reshape(bf16[640,2304]{1,0:T(8,128)(2,1)} %slice.190) | data formatting | bytes 5898240 | tf_op jit(solution)/shard_map/reshape;reshape | solution.py:26
  162.5 5.6 reshape.397
  168.2 12.1 %reshape.399 = bf16[4,200,3,12,64]{4,3,2,1,0:T(8,128)(2,1)} reshape(bf16[800,2304]{1,0:T(8,128)(2,1)} %slice.186) | data formatting | bytes 7372800 | tf_op jit(solution)/shard_map/reshape;reshape | solution.py:26
  180.2 7.1 fusion.136
  239.4 14.1 %fusion.135 = (bf16[32,1152,64]{1,2,0:T(8,128)(2,1)}, bf16[32,1152,64]{1,2,0:T(8,128)(2,1)}) fusion(bf16[32,2592,64]{1,2,0:T(8,128)(2,1)} %all-gather.13.cloned.1.call-done), kind=kLoop, calls=%fused_computation.187 | loop fusion | bytes 18874368 | tf_op jit(solution)/shard_map/slice | solution.py:80
  253.5 9.7 %copy.225 = bf16[32,1152,64]{2,1,0:T(8,128)(2,1)} copy(bf16[32,1152,64]{1,2,0:T(8,128)(2,1)} %get-tuple-element.93) | data formatting | bytes 9437184 | tf_op jit(solution)/shard_map/slice | solution.py:80
  263.2 15.5 %reshape.361 = bf16[8,4,384,192]{3,2,1,0:T(8,128)(2,1)} reshape(bf16[32,1152,64]{2,1,0:T(8,128)(2,1)} %copy.225) | data formatting | bytes 9437184 | tf_op jit(solution)/shard_map/reshape | solution.py:80
  278.7 8.8 copy.226
  287.5 5.6 copy.276
  293.1 9.7 %copy.221 = bf16[32,1152,64]{2,1,0:T(8,128)(2,1)} copy(bf16[32,1152,64]{1,2,0:T(8,128)(2,1)} %get-tuple-element.94) | data formatting | bytes 9437184 | tf_op jit(solution)/shard_map/slice | solution.py:80
  302.8 13.4 %reshape.359 = bf16[8,4,96,768]{3,2,1,0:T(8,128)(2,1)} reshape(bf16[32,1152,64]{2,1,0:T(8,128)(2,1)} %copy.221) | data formatting | bytes 9437184 | tf_op jit(solution)/shard_map/reshape | solution.py:80
  316.2 6.0 copy.222
  327.7 48.3 %multiply_convert_fusion = (bf16[1440,3072]{1,0:T(8,128)(2,1)}, f32[1440,3072]{1,0:T(8,128)}, f32[1440,3072]{1,0:T(8,128)}) fusion(f32[3072]{0:T(1024)S(1)} %reshape.382, bf16[768,3072]{1,0:T(8,128)(2,1)S(1)} %bitcast.187, f32[1440,768]{1,0:T(8,128)S(1)} %get-tuple-element.124, f32[768]{0:T(1024)S(1)} %reshape.381, f32[768]{0:T(1024)S(1)} %reshape.380, ...), kind=kOutput, calls=%fused_computation.6 | convolution fusion | flops 7092264960 | bytes 53409024 | tf_op jit(solution)/shard_map/dot_general | solution.py:173
  376.1 20.8 %convert_reduce_fusion = (f32[3072]{0:T(1024)S(1)}, bf16[1440,3072]{1,0:T(8,128)(2,1)}) fusion(f32[1440,3072]{1,0:T(8,128)} %get-tuple-element.92, bf16[3072,768]{0,1:T(8,128)(2,1)S(1)} %bitcast.186, bf16[640,768]{1,0:T(8,128)(2,1)} %bitcast.189, bf16[800,768]{1,0:T(8,128)(2,1)S(1)} %bitcast.179, f32[1440,3072]{1,0:T(8,128)} %get-tuple-element.125, ...), kind=kOutput, calls=%fused_computation.4 | convolution fusion | flops 6874395648 | bytes 51191808 | tf_op jit(solution)/shard_map/tj,ij->ti/dot_general | solution.py:182
  396.8 13.5 %multiply_reduce_fusion.1 = (f32[768]{0:T(1024)}, f32[1440]{0:T(1024)S(1)}, f32[768]{0:T(1024)S(1)}, f32[1440,768]{1,0:T(8,128)S(1)}) fusion(f32[1440,768]{1,0:T(8,128)S(1)} %get-tuple-element.124, f32[1440]{0:T(1024)S(1)} %fusion.104, f32[1440]{0:T(1024)S(1)} %broadcast_multiply_fusion, f32[768]{0:T(1024)S(1)} %reshape.380, ...), kind=kOutput, calls=%fused_computation.67 | convolution fusion | flops 6803616768 | bytes 22439808 | tf_op jit(solution)/shard_map/tj,ij->ti/dot_general | solution.py:187
  429.5 10.1 %convert_bitcast_fusion.2 = bf16[16,40,1,12,64]{4,1,3,0,2:T(8,128)(2,1)} fusion(f32[16,12,40,40]{2,3,1,0:T(8,128)} %fusion.100, f32[16,12,40,40]{2,3,1,0:T(8,128)} %copy-done.7, f32[16,12,40]{2,1,0:T(8,128)S(1)} %copy-done.34, bf16[16,40,1,12,64]{4,3,2,1,0:T(8,128)(2,1)} %copy-done.26), kind=kOutput, calls=%fused_computation.98 | convolution fusion | flops 41971240 | bytes 4454400 | tf_op jit(solution)/shard_map/chqk,ckhd->cqhd/dot_general | solution.py:59
  439.6 9.1 %convert_bitcast_fusion.1 = bf16[16,40,1,12,64]{4,1,3,0,2:T(8,128)(2,1)} fusion(f32[16,12,40,40]{2,3,1,0:T(8,128)} %fusion.100, f32[16,12,40,40]{2,3,1,0:T(8,128)} %copy-done.7, f32[16,12,40]{2,1,0:T(8,128)S(1)} %copy-done.34, bf16[16,40,1,12,64]{4,3,2,1,0:T(8,128)(2,1)S(1)} %copy-done.25), kind=kOutput, calls=%fused_computation.97 | convolution fusion | flops 41971240 | bytes 4454400 | tf_op jit(solution)/shard_map/chqk,cqhd->ckhd/dot_general | solution.py:62
  455.8 7.3 fusion.81
  463.1 7.3 fusion.97
  470.4 19.7 %fusion.92 = bf16[4,200,1,12,64]{1,4,3,0,2:T(8,128)(2,1)} fusion(f32[4,12,200,200]{2,3,1,0:T(8,128)} %fusion.81, f32[4,12,200]{2,1,0:T(8,128)S(1)} %copy-done.44, f32[4,12,200,200]{2,3,1,0:T(8,128)} %copy-done.3, pred[4,200]{1,0:T(4,128)(4,1)S(1)} %copy-done.50, bf16[4,200,1,12,64]{1,4,3,0,2:T(8,128)(2,1)S(1)} %copy-done.15), kind=kOutput, calls=%fused_computation.122 | convolution fusion | flops 267504192 | bytes 17856800 | tf_op jit(solution)/shard_map/chqk,ckhd->cqhd/dot_general | solution.py:59
  490.1 19.4 %fusion.87 = bf16[4,200,1,12,64]{1,4,3,0,2:T(8,128)(2,1)} fusion(f32[4,12,200,200]{2,3,1,0:T(8,128)} %fusion.81, f32[4,12,200]{2,1,0:T(8,128)S(1)} %copy-done.44, f32[4,12,200,200]{2,3,1,0:T(8,128)} %copy-done.3, pred[4,200]{1,0:T(4,128)(4,1)S(1)} %copy-done.50, bf16[4,200,1,12,64]{1,4,3,0,2:T(8,128)(2,1)} %copy.264), kind=kOutput, calls=%fused_computation.121 | convolution fusion | flops 267504192 | bytes 17856800 | tf_op jit(solution)/shard_map/chqk,cqhd->ckhd/dot_general | solution.py:62
  509.5 5.9 pad_maximum_fusion.2
  515.4 12.7 %copy.254 = bf16[16,40,3,12,64]{1,0,4,3,2:T(8,128)(2,1)} copy(bf16[16,40,3,12,64]{4,1,3,0,2:T(8,128)(2,1)} %pad_maximum_fusion.2) | data formatting | bytes 5898240 | tf_op jit(solution)/shard_map/convert_element_type | solution.py:69
  528.1 14.1 %reshape.398 = bf16[640,2304]{0,1:T(8,128)(2,1)} reshape(bf16[16,40,3,12,64]{1,0,4,3,2:T(8,128)(2,1)} %copy.254) | data formatting | bytes 5898240 | tf_op jit(solution)/shard_map/convert_element_type | solution.py:69
  544.7 6.6 copy.235
  551.3 9.6 %convert_element_type.280 = bf16[800,2304]{0,1:T(8,128)(2,1)} reshape(bf16[4,200,3,12,64]{1,0,4,3,2:T(4,128)(2,1)} %copy.235) | data formatting | bytes 7372800 | tf_op jit(solution)/shard_map/convert_element_type | solution.py:69
  560.9 6.7 convert_reduce_fusion.1
  567.7 14.5 %fusion.131 = (f32[768]{0:T(1024)S(1)}, f32[1440]{0:T(1024)S(1)}, f32[1440,768]{1,0:T(8,128)S(1)}) fusion(f32[768]{0:T(1024)S(1)} %copy-done.48, f32[1440]{0:T(1024)S(1)} %copy-done.37, bf16[640,768]{1,0:T(8,128)(2,1)S(1)} %bitcast.173, bf16[800,768]{1,0:T(8,128)(2,1)S(1)} %bitcast.155, bf16[768,2304]{1,0:T(8,128)(2,1)} %reshape.351, ...), kind=kOutput, calls=%fused_computation.185 | convolution fusion | flops 5119301120 | bytes 16827648 | tf_op jit(solution)/shard_map/tj,ij->ti/dot_general | solution.py:210
  608.9 12.4 %convolution_convert_fusion = bf16[768,2304]{1,0:T(8,128)(2,1)} fusion(bf16[640,2304]{0,1:T(8,128)(2,1)} %reshape.398, bf16[800,2304]{0,1:T(8,128)(2,1)} %convert_element_type.280, f32[768]{0:T(1024)S(1)} %copy-done.52, f32[768]{0:T(1024)S(1)} %copy-done.48, f32[1440]{0:T(1024)S(1)} %copy-done.39, f32[1440]{0:T(1024)S(1)} %copy-done.37, ...), kind=kOutput, calls=%fused_computation.48 | convolution fusion | flops 5121073152 | bytes 12403968 | tf_op jit(solution)/shard_map/ti,tj->ij/dot_general | solution.py:203
  621.3 9.1 %reshape.369 = bf16[8,96,4,576]{3,2,1,0:T(4,128)(2,1)} reshape(bf16[768,2304]{1,0:T(8,128)(2,1)} %convolution_convert_fusion) | data formatting | bytes 7077888 | tf_op jit(solution)/shard_map/reshape | solution.py:95
  635.0 8.0 reshape.370
  649.1 13.2 %convolution_convert_fusion.1 = bf16[3072,768]{1,0:T(8,128)(2,1)} fusion(bf16[1440,3072]{1,0:T(8,128)(2,1)} %get-tuple-element.91, bf16[640,768]{1,0:T(8,128)(2,1)S(1)} %bitcast.192, bf16[800,768]{1,0:T(8,128)(2,1)S(1)} %bitcast.182), kind=kOutput, calls=%fused_computation.49 | convolution fusion | flops 6801555456 | bytes 15777792 | tf_op jit(solution)/shard_map/ti,tj->ij/dot_general | solution.py:180
  662.3 6.7 copy.244
  669.1 5.9 copy.277
  675.0 13.5 %convolution_convert_fusion.2 = bf16[768,3072]{1,0:T(8,128)(2,1)} fusion(bf16[1440,3072]{1,0:T(8,128)(2,1)} %get-tuple-element.129, f32[1440,768]{1,0:T(8,128)S(1)} %bitcast.166, f32[768]{0:T(1024)S(1)} %copy-done.54, f32[768]{0:T(1024)S(1)} %reshape.380, f32[1440]{0:T(1024)S(1)} %fusion.104, f32[1440]{0:T(1024)S(1)} %broadcast_multiply_fusion), kind=kOutput, calls=%fused_computation.50 | convolution fusion | flops 6802661376 | bytes 18007296 | tf_op jit(solution)/shard_map/ti,tj->ij/dot_general | solution.py:185
  688.5 9.8 %reshape.373 = bf16[8,96,4,768]{3,2,1,0:T(4,128)(2,1)} reshape(bf16[768,3072]{1,0:T(8,128)(2,1)} %convolution_convert_fusion.2) | data formatting | bytes 9437184 | tf_op jit(solution)/shard_map/reshape | solution.py:95
  703.6 9.3 %reshape.374 = bf16[32,576,128]{2,1,0:T(8,128)(2,1)} reshape(bf16[8,4,96,768]{3,2,1,0:T(8,128)(2,1)} %bitcast.162) | data formatting | bytes 9437184 | tf_op jit(solution)/shard_map/reshape | solution.py:96
  712.9 9.1 %copy.245 = bf16[8,4,384,192]{3,2,1,0:T(8,128)(2,1)} copy(bf16[8,4,384,192]{2,0,3,1:T(8,128)(2,1)} %bitcast.163) | data formatting | bytes 9437184 | tf_op jit(solution)/shard_map/transpose | solution.py:95
  722.1 12.2 %reshape.376 = bf16[32,576,128]{2,1,0:T(8,128)(2,1)} reshape(bf16[8,4,384,192]{3,2,1,0:T(8,128)(2,1)} %copy.245) | data formatting | bytes 9437184 | tf_op jit(solution)/shard_map/reshape | solution.py:96
  734.2 7.7 pad_maximum_fusion
  743.0 13.1 %add_convert_fusion.2 = bf16[1440,768]{1,0:T(8,128)(2,1)S(1)} fusion(f32[1440,768]{1,0:T(8,128)} %copy-done.6, bf16[1440,3072]{1,0:T(8,128)(2,1)} %get-tuple-element.91, bf16[3072,768]{0,1:T(8,128)(2,1)} %bitcast.183, f32[768]{0:T(1024)S(1)} %reshape.383), kind=kOutput, calls=%fused_computation.71 | convolution fusion | flops 6798090240 | bytes 20204544 | tf_op jit(solution)/shard_map/dot_general | solution.py:176
  767.1 130.3 %reduce-scatter.5.cloned.1.call-done = bf16[1,1152,128]{2,1,0:T(8,128)(2,1)} async-done(((bf16[32,1152,128]{2,1,0:T(8,128)(2,1)}), bf16[1,1152,128]{2,1,0:T(8,128)(2,1)}) %reduce-scatter.5.cloned.1.call-update) | async-done | bytes 294928 | tf_op jit(solution)/shard_map/reduce_scatter | solution.py:98
  (280 shorter events, 191.0 us)
Async XLA Ops:
  7.2 15.2 %copy-start = (s32[64,40]{0,1:T(8,128)S(1)}, s32[64,40]{0,1:T(8,128)}, u32[]{:S(2)}) copy-start(s32[64,40]{0,1:T(8,128)} %param.21) | copy-start | bytes 30724
  7.2 15.3 %copy-start.9 = (bf16[16,40,768]{2,1,0:T(8,128)(2,1)S(1)}, bf16[16,40,768]{2,1,0:T(8,128)(2,1)}, u32[]{:S(2)}) copy-start(bf16[16,40,768]{2,1,0:T(8,128)(2,1)} %param.19) | copy-start | bytes 2949124
  7.2 15.3 %copy-start.4 = (bf16[4,200,768]{2,1,0:T(8,128)(2,1)S(1)}, bf16[4,200,768]{2,1,0:T(8,128)(2,1)}, u32[]{:S(2)}) copy-start(bf16[4,200,768]{2,1,0:T(8,128)(2,1)} %param.18) | copy-start | bytes 3686404
  7.2 73.8 %all-gather.11.cloned.1.call-start = ((), (), s32[]{:S(2)}) async-start(), calls=%async_computation.5 | async-start | bytes 4325376 | tf_op jit(solution)/shard_map/all_gather | solution.py:76
  16.0 205.1 %all-gather.13.cloned.1.call-start = ((), (), s32[]{:S(2)}) async-start(), calls=%async_computation.6 | async-start | bytes 11354112 | tf_op jit(solution)/shard_map/all_gather | solution.py:76
  22.3 738.0 %all-gather.9.cloned.1.call-start = ((), (), s32[]{:S(2)}) async-start(), calls=%async_computation.4 | async-start | bytes 1216512 | tf_op jit(solution)/shard_map/all_gather | solution.py:225
  23.6 185.1 %copy-start.49 = (pred[4,200]{1,0:T(4,128)(4,1)}, pred[4,200]{1,0:T(4,128)(4,1)S(1)}, u32[]{:S(2)}) copy-start(pred[4,200]{1,0:T(4,128)(4,1)S(1)} %dynamic-slice_compare_fusion) | copy-start | bytes 2404
  23.6 98.0 %copy-start.36 = (f32[1440]{0:T(1024)}, f32[1440]{0:T(1024)S(1)}, u32[]{:S(2)}) copy-start(f32[1440]{0:T(1024)S(1)} %broadcast_multiply_fusion.1) | copy-start | bytes 17284
  25.1 96.6 %copy-start.38 = (f32[1440]{0:T(1024)}, f32[1440]{0:T(1024)S(1)}, u32[]{:S(2)}) copy-start(f32[1440]{0:T(1024)S(1)} %fusion.103) | copy-start | bytes 17284
  84.5 37.2 %copy-start.51 = (f32[768]{0:T(1024)}, f32[768]{0:T(1024)S(1)}, u32[]{:S(2)}) copy-start(f32[768]{0:T(1024)S(1)} %reshape.378) | copy-start | bytes 9220
  84.7 37.0 %copy-start.47 = (f32[768]{0:T(1024)}, f32[768]{0:T(1024)S(1)}, u32[]{:S(2)}) copy-start(f32[768]{0:T(1024)S(1)} %reshape.377) | copy-start | bytes 9220
  136.0 191.6 %copy-start.53 = (f32[768]{0:T(1024)}, f32[768]{0:T(1024)S(1)}, u32[]{:S(2)}) copy-start(f32[768]{0:T(1024)S(1)} %reshape.381) | copy-start | bytes 9220
  324.2 51.9 %slice-start.4 = ((s8[4718592]{0:T(1024)(128)(4,1)}), s8[524288]{0:T(1024)(128)(4,1)S(1)}, s32[]{:S(2)}) async-start(s8[4718592]{0:T(1024)(128)(4,1)} %bitcast.184), calls=%async_computation.11 | async-start | bytes 1048576
  327.0 83.3 %copy-start.6 = (f32[1440,768]{1,0:T(8,128)}, f32[1440,768]{1,0:T(8,128)S(1)}, u32[]{:S(2)}) copy-start(f32[1440,768]{1,0:T(8,128)S(1)} %get-tuple-element.124) | copy-start | bytes 13271044
  327.7 48.4 %copy-start.42 = (f32[1440]{0:T(1024)}, f32[1440]{0:T(1024)S(1)}, u32[]{:S(2)}) copy-start(f32[1440]{0:T(1024)S(1)} %multiply_reduce_fusion.3) | copy-start | bytes 17284
  327.7 48.3 %copy-start.17 = (bf16[4,200,768]{2,1,0:T(8,128)(2,1)S(1)}, bf16[4,200,768]{2,1,0:T(8,128)(2,1)}, u32[]{:S(2)}) copy-start(bf16[4,200,768]{2,1,0:T(8,128)(2,1)} %param.34) | copy-start | bytes 3686404
  327.7 48.3 %slice-start.5 = ((s8[4718592]{0:T(1024)(128)(4,1)}), s8[4194304]{0:T(1024)(128)(4,1)S(1)}, s32[]{:S(2)}) async-start(s8[4718592]{0:T(1024)(128)(4,1)} %bitcast.184), calls=%async_computation.12 | async-start | bytes 8388608
  396.8 13.5 %copy-start.43 = (f32[1440]{0:T(1024)S(1)}, f32[1440]{0:T(1024)}, u32[]{:S(2)}) copy-start(f32[1440]{0:T(1024)} %copy-done.42) | copy-start | bytes 17284
  422.1 5.0 copy-start.8
  422.1 5.0 copy-start.34
  429.5 10.1 %copy-start.25 = (bf16[16,40,1,12,64]{4,3,2,1,0:T(8,128)(2,1)S(1)}, bf16[16,40,1,12,64]{4,3,2,1,0:T(8,128)(2,1)}, u32[]{:S(2)}) copy-start(bf16[16,40,1,12,64]{4,3,2,1,0:T(8,128)(2,1)} %copy-done.24) | copy-start | bytes 2949124
  455.8 7.3 copy-start.16
  455.8 7.3 copy-start.44
  455.8 7.3 copy-start.50
  463.1 7.3 copy-start.15
  490.1 19.4 %copy-start.13 = (bf16[16,40,1,12,64]{4,1,3,0,2:T(8,128)(2,1)S(1)}, bf16[16,40,1,12,64]{4,1,3,0,2:T(8,128)(2,1)}, u32[]{:S(2)}) copy-start(bf16[16,40,1,12,64]{4,1,3,0,2:T(8,128)(2,1)} %convert_bitcast_fusion) | copy-start | bytes 2949124
  528.1 14.2 %copy-start.28 = (bf16[4,200,1,12,64]{1,4,3,0,2:T(8,128)(2,1)S(1)}, bf16[4,200,1,12,64]{1,4,3,0,2:T(8,128)(2,1)}, u32[]{:S(2)}) copy-start(bf16[4,200,1,12,64]{1,4,3,0,2:T(8,128)(2,1)} %fusion.97) | copy-start | bytes 3686404
  528.1 14.2 %copy-start.29 = (bf16[4,200,1,12,64]{1,4,3,0,2:T(8,128)(2,1)S(1)}, bf16[4,200,1,12,64]{1,4,3,0,2:T(8,128)(2,1)}, u32[]{:S(2)}) copy-start(bf16[4,200,1,12,64]{1,4,3,0,2:T(8,128)(2,1)} %fusion.92) | copy-start | bytes 3686404
  560.9 6.7 copy-start.5
  560.9 6.7 copy-start.10
  560.9 6.7 copy-start.37
  560.9 6.7 copy-start.48
  560.9 25.5 %slice-start = ((s8[4423680]{0:T(1024)(128)(4,1)}), s8[4194304]{0:T(1024)(128)(4,1)S(1)}, s32[]{:S(2)}) async-start(s8[4423680]{0:T(1024)(128)(4,1)} %bitcast.148), calls=%async_computation.7 | async-start | bytes 8388608
  567.6 14.6 %copy-start.41 = (f32[1440]{0:T(1024)S(1)}, f32[1440]{0:T(1024)}, u32[]{:S(2)}) copy-start(f32[1440]{0:T(1024)} %copy-done.40) | copy-start | bytes 17284
  567.6 14.6 %copy-start.39 = (f32[1440]{0:T(1024)S(1)}, f32[1440]{0:T(1024)}, u32[]{:S(2)}) copy-start(f32[1440]{0:T(1024)} %copy-done.38) | copy-start | bytes 17284
  567.7 18.7 %slice-start.1 = ((s8[4423680]{0:T(1024)(128)(4,1)}), s8[229376]{0:T(1024)(128)(4,1)S(1)}, s32[]{:S(2)}) async-start(s8[4423680]{0:T(1024)(128)(4,1)} %bitcast.148), calls=%async_computation.8 | async-start | bytes 458752
  582.2 4.1 copy-start.45
  582.2 4.2 copy-start.18
  582.2 4.2 copy-start.22
  586.4 4.6 copy-start.55
  591.7 172.2 %reduce-scatter.3.cloned.1.call-start = ((), (), s32[]{:S(2)}) async-start(), calls=%async_computation.2 | async-start | bytes 4866048 | tf_op jit(solution)/shard_map/reduce_scatter | solution.py:98
  597.1 11.8 %copy-start.52 = (f32[768]{0:T(1024)S(1)}, f32[768]{0:T(1024)}, u32[]{:S(2)}) copy-start(f32[768]{0:T(1024)} %copy-done.51) | copy-start | bytes 9220
  635.0 8.0 copy-start.19
  647.9 249.4 %reduce-scatter.5.cloned.1.call-start = ((), (), s32[]{:S(2)}) async-start(), calls=%async_computation.3 | async-start | bytes 9732096 | tf_op jit(solution)/shard_map/reduce_scatter | solution.py:98
  662.3 12.7 %slice-start.2 = ((s8[4423680]{0:T(1024)(128)(4,1)}), s8[229376]{0:T(1024)(128)(4,1)S(1)}, s32[]{:S(2)}) async-start(s8[4423680]{0:T(1024)(128)(4,1)} %bitcast.165), calls=%async_computation.9 | async-start | bytes 458752
  669.1 5.9 slice-start.3
  669.1 5.9 copy-start.54
  758.2 141.9 %copy-start.1 = (s32[64,40]{0,1:T(8,128)S(1)}, s32[64,40]{0,1:T(8,128)}, u32[]{:S(2)}) copy-start(s32[64,40]{0,1:T(8,128)} %param.21) | copy-start | bytes 30724
  (19 other events, 40.3 us)
Sparse Core Ops, SparseCore 0:
  16.2 64.7 all-gather.10
  84.4 87.4 all-gather.12
  591.8 52.6 all-gather.8
  649.9 105.8 reduce-scatter.2
  762.5 134.7 reduce-scatter.4
